TPU v7x, 256 devices: a whole 4x4x8 slice. The times are simulated.
256 devices in a mesh: row: 16 (over z_lo, x, core), col: 16 (over z_hi, y).
Axes of the slice: x: 4, y: 4, z: 8 (z_hi: 4, z_lo: 2; z = z_hi * 2 + z_lo), core: 2. Of those that a mesh axis runs over, the one named last changes fastest.
Arguments:
- blocks_inverse: bfloat16 [12288, 12288], P('row', 'col'), as said below
- factor_rows: bfloat16 [2, 6144, 256], P(None, 'row'), may hold values from -0.15234375 to 0.15234375
- block_lists: int32 [2, 48], replicated, may hold values from 0 to 95, as said below
- diag_inverse: float32 [2, 256, 256], replicated, as said below
Outputs:
- column_inverse: float32 [2, 12288, 256], P(None, 'row')
- mirror_inverse: float32 [2, 256, 12288], P(None, None, 'col')
- diagonal_inverse: float32 [2, 256, 256], replicated
Inputs may be any that keep to these rules, and one draw needn't show every extreme that they name: blocks_inverse is exactly symmetric and positive definite. block_lists[s, m] is 2 * m or 2 * m + 1. diag_inverse[s] is symmetric.
All inputs are finite; a program needn't handle non-finite values.
Results may differ from a plain program's by a relative error of at most 0.0003.
Values may be sent and summed in bfloat16 or wider, within the bound.
A program may use at most 64 MiB of HBM per device.

v0:
```python
import jax
import jax.numpy as jnp
from jax import lax
from jax.sharding import PartitionSpec as P

BS = 128


def broadcast(x, axis, root):
    mine = lax.axis_index(axis) == root
    return lax.psum(jnp.where(mine, x, jnp.zeros_like(x)), axis)


def pair_bits(block_lists, first_block, block_count):
    local_lists = lax.dynamic_slice_in_dim(block_lists, first_block // 2, block_count // 2, 1)
    pair_first = 2 * (first_block // 2 + jnp.arange(block_count // 2, dtype=jnp.int32))
    return local_lists - pair_first[None, :]


def expand_pairs(packed, bits):
    sup_count = packed.shape[0]
    feature_count = packed.shape[2]
    pairs = bits.shape[1]
    grouped = packed.reshape(sup_count, pairs, 1, BS, feature_count)
    which = (
        bits[:, :, None, None, None] == jnp.arange(2, dtype=jnp.int32)[None, None, :, None, None]
    )
    dense = jnp.where(which, grouped, jnp.zeros((), packed.dtype))
    return dense.reshape(sup_count, pairs * 2 * BS, feature_count)


def compact_pairs(dense, bits):
    sup_count = dense.shape[0]
    feature_count = dense.shape[2]
    pairs = bits.shape[1]
    grouped = dense.reshape(sup_count, pairs, 2, BS, feature_count)
    chosen = jnp.where(bits[:, :, None, None] == 0, grouped[:, :, 0], grouped[:, :, 1])
    return chosen.reshape(sup_count, pairs * BS, feature_count)


def multiply_each(matrix, stacked):
    results = []
    for sup_index in range(stacked.shape[0]):
        results.append(
            jnp.dot(matrix, stacked[sup_index].astype(jnp.float32), precision=lax.Precision.HIGHEST)
        )
    return jnp.stack(results)


def local(blocks_inverse, factor_rows, block_lists, diag_inverse):
    row_index = lax.axis_index("row")
    col_index = lax.axis_index("col")
    row_blocks = blocks_inverse.shape[0] // BS
    col_blocks = blocks_inverse.shape[1] // BS
    row_bits = pair_bits(block_lists, row_index * row_blocks, row_blocks)
    col_bits = pair_bits(block_lists, col_index * col_blocks, col_blocks)
    packed_length = col_blocks // 2 * BS
    root_row = col_index * col_blocks // row_blocks
    gathered = lax.all_gather(factor_rows, "row", axis=1, tiled=True)
    column_packed = lax.dynamic_slice_in_dim(gathered, col_index * packed_length, packed_length, 1)
    column_dense = expand_pairs(column_packed, col_bits)
    blocks_wide = blocks_inverse.astype(jnp.float32)
    products = multiply_each(blocks_wide, column_dense)
    listed_products = compact_pairs(products, row_bits)
    diagonal_terms = jnp.einsum(
        "srw,srv->swv",
        factor_rows.astype(jnp.float32),
        listed_products,
        precision=lax.Precision.HIGHEST,
    )
    diagonal_inverse = diag_inverse + lax.psum(diagonal_terms, ("row", "col"))
    row_total = lax.psum(listed_products, "col")
    column_inverse = -expand_pairs(row_total, row_bits)
    mirror_total = broadcast(row_total, "row", root_row)
    mirror_inverse = jnp.transpose(-expand_pairs(mirror_total, col_bits), (0, 2, 1))
    return (column_inverse, mirror_inverse, diagonal_inverse)


def solution(mesh):
    return jax.shard_map(
        local,
        mesh=mesh,
        in_specs=(P("row", "col"), P(None, "row", None), P(), P()),
        out_specs=(P(None, "row", None), P(None, None, "col"), P()),
        check_vma=False,
    )
```

profile of v0, /device:TPU:1, one launch (start us, length us, event | category | flops | bytes accessed | tf_op | source)
XLA Modules:
  0.0 641.8 jit_solution(4474671392308871341)
XLA Ops:
  7.2 0.0 copy-start
  7.2 0.0 all-gather.2.cloned.1.call-start
  7.2 0.7 all-gather.2.cloned.1.call-update
  8.0 0.8 broadcast_compare_fusion
  8.7 0.1 broadcast_bitcast_fusion
  8.8 0.8 dynamic-slice_subtract_fusion
  9.6 0.1 iota_compare_fusion
  9.6 49.3 %all-gather.2.cloned.1.call-done = bf16[2,6144,256]{2,1,0:T(8,128)(2,1)} async-done(((bf16[2,384,256]{2,1,0:T(8,128)(2,1)}), bf16[2,6144,256]{2,1,0:T(8,128)(2,1)}) %all-gather.2.cloned.1.call-update) | async-done | bytes 6291472 | tf_op jit(solution)/shard_map/all_gather | solution.py:59
  59.0 1.0 constant_dynamic-slice_fusion
  60.0 0.1 broadcast_select_fusion
  60.1 0.8 fusion.1
  60.9 0.5 convolution_bitcast_fusion.1
  61.4 0.4 stack.9
  61.9 1.5 convolution_bitcast_fusion
  63.4 0.4 stack.10
  63.8 0.3 constant_dynamic-update-slice_fusion.1
  64.1 0.3 constant_dynamic-update-slice_fusion
  64.4 1.2 fusion
  65.6 1.0 copy.11
  66.6 1.0 copy.10
  67.6 0.2 broadcast_select_fusion.2
  67.8 0.0 copy-start.1
  67.8 3.0 convolution_bitcast_fusion.2
  70.8 0.7 all-reduce.4.cloned.1.call-update
  71.5 0.0 copy-start.3
  71.5 0.0 all-reduce.8.cloned.1.call-start
  71.6 0.7 all-reduce.8.cloned.1.call-update
  72.2 0.0 all-reduce.6.cloned.1.call-start
  72.3 160.2 %all-reduce.4.cloned.1.call-done = f32[2,384,256]{2,1,0:T(8,128)} async-done(((f32[2,384,256]{2,1,0:T(8,128)}), f32[2,384,256]{2,1,0:T(8,128)}) %all-reduce.4.cloned.1.call-update) | async-done | bytes 786448 | tf_op jit(solution)/shard_map/psum | solution.py:72
  232.5 0.9 broadcast_select_fusion.1
  233.5 0.0 all-reduce.6.cloned.1.call-update
  233.5 0.1 iota_compare_fusion.1
  233.6 0.1 broadcast_in_dim.93
  233.7 0.1 broadcast_in_dim.107
  233.8 0.2 copy.15
  234.0 267.5 %all-reduce.8.cloned.1.call-done = f32[2,256,256]{1,2,0:T(8,128)} async-done(((f32[2,256,256]{1,2,0:T(8,128)}), f32[2,256,256]{1,2,0:T(8,128)}) %all-reduce.8.cloned.1.call-update) | async-done | bytes 524304 | tf_op jit(solution)/shard_map/psum | solution.py:71
  501.5 1.1 add.48
  502.6 1.0 copy.17
  503.6 0.4 copy.12
  504.0 1.7 broadcast_in_dim.104
  505.7 2.5 broadcast_in_dim.105
  508.2 1.3 select_negate_fusion
  509.5 3.0 copy.16
  512.5 115.7 %all-reduce.6.cloned.1.call-done = f32[2,3,128,256]{3,2,1,0:T(8,128)} async-done(((f32[2,3,128,256]{3,2,1,0:T(8,128)}), f32[2,3,128,256]{3,2,1,0:T(8,128)}) %all-reduce.6.cloned.1.call-update) | async-done | bytes 786448 | tf_op jit(solution)/shard_map/psum | solution.py:11
  628.2 1.5 copy.13
  629.8 1.7 broadcast_in_dim.112
  631.4 2.5 broadcast_in_dim.113
  634.0 1.3 negate_bitcast_fusion
  (11 shorter events, 0.1 us)
Async XLA Ops:
  7.2 53.8 %copy-start = (bf16[768,768]{1,0:T(8,128)(2,1)S(1)}, bf16[768,768]{1,0:T(8,128)(2,1)}, u32[]{:S(2)}) copy-start(bf16[768,768]{1,0:T(8,128)(2,1)} %param.4) | copy-start | bytes 3538948
  7.2 51.8 %all-gather.2.cloned.1.call-start = ((), (), s32[]{:S(2)}) async-start(), calls=%async_computation | async-start | bytes 6684672 | tf_op jit(solution)/shard_map/all_gather | solution.py:59
  67.8 3.0 copy-start.1
  70.8 161.8 %all-reduce.4.cloned.1.call-start = ((), (), s32[]{:S(2)}) async-start(), calls=%async_computation.1 | async-start | bytes 1572864 | tf_op jit(solution)/shard_map/psum | solution.py:72
  71.5 162.3 %copy-start.3 = (f32[2,256,256]{2,1,0:T(8,128)S(1)}, f32[2,256,256]{2,1,0:T(8,128)}, u32[]{:S(2)}) copy-start(f32[2,256,256]{2,1,0:T(8,128)} %param.7) | copy-start | bytes 1572868
  71.5 430.0 %all-reduce.8.cloned.1.call-start = ((), (), s32[]{:S(2)}) async-start(), calls=%async_computation.3 | async-start | bytes 1048576 | tf_op jit(solution)/shard_map/psum | solution.py:71
  72.2 556.0 %all-reduce.6.cloned.1.call-start = ((), (), s32[]{:S(2)}) async-start(), calls=%async_computation.2 | async-start | bytes 1572864 | tf_op jit(solution)/shard_map/psum | solution.py:11
  234.0 269.6 %copy-start.2 = (f32[2,384,256]{2,1,0:T(8,128)S(1)}, f32[2,384,256]{2,1,0:T(8,128)}, u32[]{:S(2)}) copy-start(f32[2,384,256]{2,1,0:T(8,128)} %all-reduce.4.cloned.1.call-done) | copy-start | bytes 2359300
Sparse Core Ops, SparseCore 0:
  9.8 49.1 all-gather.1
  74.8 157.7 all-reduce.3
  238.6 262.8 all-reduce.7
  504.0 124.2 all-reduce.5
where the time goes:
time: 642 us
  waiting for transfers between devices  595 us (93%)
  local copies, waits for them, and re-layouts  21.3 us (3%)
  between operations  14 us (2%)
  other arithmetic  6.57 us (1%)
    psum x1, waiting for transfers between devices, local(): diagonal_inverse = diag_inverse + lax.psum(diagonal_terms, ('row', 'col'))  268 us
    psum x1, waiting for transfers between devices, local(): row_total = lax.psum(listed_products, 'col')  160 us
    psum x1, waiting for transfers between devices, broadcast(): return lax.psum(jnp.where(mine, x, jnp.zeros_like(x)), axis)  116 us
    all_gather x1, waiting for transfers between devices, local(): gathered = lax.all_gather(factor_rows, 'row', axis=1, tiled=True)  49.3 us
  transfers between devices with their start and end apart: 4, of which 4 were waited for; matrix products, arithmetic and copies ran while one was open for 2% of the time, Pallas kernels for 0%

commit v1 on v0

--- a/solution.py
+++ b/solution.py
@@ -68,7 +68,7 @@
         listed_products,
         precision=lax.Precision.HIGHEST,
     )
-    diagonal_inverse = diag_inverse + lax.psum(diagonal_terms, ("row", "col"))
+    diagonal_inverse = diag_inverse + lax.psum(lax.psum(diagonal_terms, "col"), "row")
     row_total = lax.psum(listed_products, "col")
     column_inverse = -expand_pairs(row_total, row_bits)
     mirror_total = broadcast(row_total, "row", root_row)

time: 642 us -> 384 us (0.60)
  waiting for transfers between devices: 595 us -> 338 us
    psum x1 -> x0, waiting for transfers between devices: 268 us -> none  [local(): diagonal_inverse = diag_inverse + lax.psum(diagonal_terms, ('row', 'col'))]
    psum x1, waiting for transfers between devices: 116 us -> 126 us  [broadcast(): return lax.psum(jnp.where(mine, x, jnp.zeros_like(x)), axis)]
  transfers between devices with their start and end apart: 4 -> 3, of which waited for: 4 -> 3; matrix products, arithmetic and copies ran while one was open for 2% -> 3% of each run, Pallas kernels for 0% -> 0%
where the time goes in v1:
time: 384 us
  waiting for transfers between devices  338 us (88%)
  local copies, waits for them, and re-layouts  21.6 us (6%)
  between operations  14 us (4%)
  other arithmetic  6.67 us (2%)
    psum x1, waiting for transfers between devices, local(): row_total = lax.psum(listed_products, 'col')  162 us
    psum x1, waiting for transfers between devices, broadcast(): return lax.psum(jnp.where(mine, x, jnp.zeros_like(x)), axis)  126 us
    all_gather x1, waiting for transfers between devices, local(): gathered = lax.all_gather(factor_rows, 'row', axis=1, tiled=True)  49.3 us
    broadcast_in_dim x9, local copies, waits for them, and re-layouts, expand_pairs(): dense = jnp.where(which, grouped, jnp.zeros((), packed.dtype))  9.01 us
  transfers between devices with their start and end apart: 3, of which 3 were waited for; matrix products, arithmetic and copies ran while one was open for 3% of the time, Pallas kernels for 0%

profile of v1, /device:TPU:1, one launch (start us, length us, event | category | flops | bytes accessed | tf_op | source)
XLA Modules:
  0.0 383.9 jit_solution(6255276534862216508)
XLA Ops:
  7.2 0.0 copy-start
  7.2 0.0 all-gather.2.cloned.1.call-start
  7.2 0.7 all-gather.2.cloned.1.call-update
  7.9 0.0 all-reduce.5.cloned.1.call-start
  8.0 0.8 broadcast_compare_fusion
  8.8 0.1 broadcast_bitcast_fusion
  8.9 0.8 dynamic-slice_subtract_fusion
  9.6 0.1 iota_compare_fusion
  9.7 49.3 %all-gather.2.cloned.1.call-done = bf16[2,6144,256]{2,1,0:T(8,128)(2,1)} async-done(((bf16[2,384,256]{2,1,0:T(8,128)(2,1)}), bf16[2,6144,256]{2,1,0:T(8,128)(2,1)}) %all-gather.2.cloned.1.call-update) | async-done | bytes 6291472 | tf_op jit(solution)/shard_map/all_gather | solution.py:59
  59.0 1.0 constant_dynamic-slice_fusion
  60.0 0.1 broadcast_select_fusion
  60.1 0.8 fusion.1
  60.9 0.5 convolution_bitcast_fusion.1
  61.4 0.4 stack.9
  61.9 1.5 convolution_bitcast_fusion
  63.4 0.4 stack.10
  63.8 0.3 constant_dynamic-update-slice_fusion.1
  64.1 0.3 constant_dynamic-update-slice_fusion
  64.4 1.2 fusion
  65.6 1.0 copy.11
  66.6 1.0 copy.10
  67.6 0.0 copy-start.3
  67.6 0.2 broadcast_select_fusion.2
  67.8 0.8 copy-done.3
  68.6 1.7 convolution_bitcast_fusion.2
  70.3 0.0 all-reduce.5.cloned.1.call-update
  70.3 0.0 copy-start.5
  70.3 0.0 all-reduce.7.cloned.1.call-start
  70.4 161.8 %all-reduce.5.cloned.1.call-done = (f32[2,384,256]{2,1,0:T(8,128)}, f32[2,256,256]{1,2,0:T(8,128)}) async-done(((f32[2,384,256]{2,1,0:T(8,128)}, f32[2,256,256]{1,2,0:T(8,128)}), (f32[2,384,256]{2,1,0:T(8,128)}, f32[2,256,256]{1,2,0:T(8,128)})) %all-reduce.5.cloned.1.call-update) | async-done | bytes 1310736 | tf_op jit(solution)/shard_map/psum | solution.py:72
  232.2 1.0 broadcast_select_fusion.1
  233.2 0.0 all-reduce.7.cloned.1.call-update
  233.2 0.1 iota_compare_fusion.1
  233.3 0.1 broadcast_in_dim.93
  233.4 0.1 broadcast_in_dim.107
  233.5 0.2 copy.15
  233.7 0.6 copy-done.2
  234.3 0.4 copy.12
  234.7 1.7 broadcast_in_dim.104
  236.4 2.5 broadcast_in_dim.105
  238.9 1.3 select_negate_fusion
  240.2 3.0 copy.16
  243.2 126.0 %all-reduce.7.cloned.1.call-done = (f32[2,3,128,256]{3,2,1,0:T(8,128)}, f32[2,256,256]{1,2,0:T(8,128)}) async-done(((f32[2,3,128,256]{3,2,1,0:T(8,128)}, f32[2,256,256]{1,2,0:T(8,128)}), (f32[2,3,128,256]{3,2,1,0:T(8,128)}, f32[2,256,256]{1,2,0:T(8,128)})) %all-reduce.7.cloned.1.call-update) | async-done | bytes 1310736 | tf_op jit(solution)/shard_map/psum | solution.py:11
  369.3 1.2 add.50
  370.4 1.0 copy.17
  371.4 0.4 copy.13
  371.8 1.7 broadcast_in_dim.112
  373.5 2.5 broadcast_in_dim.113
  376.1 1.3 negate_bitcast_fusion
  (12 shorter events, 0.1 us)
Async XLA Ops:
  7.2 53.8 %copy-start = (bf16[768,768]{1,0:T(8,128)(2,1)S(1)}, bf16[768,768]{1,0:T(8,128)(2,1)}, u32[]{:S(2)}) copy-start(bf16[768,768]{1,0:T(8,128)(2,1)} %param.4) | copy-start | bytes 3538948
  7.2 51.8 %all-gather.2.cloned.1.call-start = ((), (), s32[]{:S(2)}) async-start(), calls=%async_computation | async-start | bytes 6684672 | tf_op jit(solution)/shard_map/all_gather | solution.py:59
  7.9 224.3 %all-reduce.5.cloned.1.call-start = ((), (), s32[]{:S(2)}) async-start(), calls=%async_computation.1 | async-start | bytes 2621440 | tf_op jit(solution)/shard_map/psum | solution.py:72
  67.6 1.0 copy-start.3
  68.6 1.7 copy-start.1
  70.3 163.2 %copy-start.5 = (f32[2,256,256]{2,1,0:T(8,128)S(1)}, f32[2,256,256]{2,1,0:T(8,128)}, u32[]{:S(2)}) copy-start(f32[2,256,256]{2,1,0:T(8,128)} %param.7) | copy-start | bytes 1572868
  70.3 298.9 %all-reduce.7.cloned.1.call-start = ((), (), s32[]{:S(2)}) async-start(), calls=%async_computation.2 | async-start | bytes 2621440 | tf_op jit(solution)/shard_map/psum | solution.py:11
  233.2 1.1 copy-start.2
  369.3 2.2 copy-start.4
Sparse Core Ops, SparseCore 0:
  9.8 49.1 all-gather.1
  70.4 161.7 all-reduce.4
  234.9 134.2 all-reduce.6
